TPU v7x, 512 devices: a whole 4x4x16 slice. The times are simulated.
512 devices in a mesh: guide: 2 (over core), patch: 256 (over x, y, z).
Axes of the slice: x: 4, y: 4, z: 16, core: 2. Of those that a mesh axis runs over, the one named last changes fastest.
Arguments:
- queries: bfloat16 [2, 28672, 128], P('guide', 'patch'), may hold values from -40 to 40
- fresh_keys: bfloat16 [2, 28672, 128], P('guide', 'patch'), may hold values from -9.5625 to 9.5625
- fresh_values: bfloat16 [2, 28672, 128], P('guide', 'patch'), may hold values from -6 to 6
- stale_keys: bfloat16 [2, 28672, 128], P('guide', 'patch'), may hold values from -10 to 10
- stale_values: bfloat16 [2, 28672, 128], P('guide', 'patch'), may hold values from -6 to 6
- hidden: bfloat16 [2, 28672, 5120], P('guide', 'patch'), may hold values from -6 to 6
- out_weight: bfloat16 [128, 5120], replicated, may hold values from -0.5 to 0.5
- modulation: float32 [5120], replicated, may hold values from 1 to 4
Outputs:
- guided: bfloat16 [28672, 5120], P('patch', 'guide')
All inputs are finite; a program needn't handle non-finite values.
Results may differ from a plain program's by a relative error of at most 0.0051.
Values may be sent and summed in bfloat16 or wider, within the bound.
No kernel may reach another device: no remote copies, remote signals or barrier semaphores. Data moves between devices by JAX's collectives and lax.ppermute only.
A program may use at most 64 MiB of HBM per device.

v0:
```python
import math

import jax
import jax.numpy as jnp
from jax import lax
from jax.sharding import PartitionSpec as P

GUIDANCE = 5.0


def swapped(value, axis, stride):
    mask = 2**stride
    pairs = [(source, source ^ mask) for source in range(lax.axis_size(axis))]
    return lax.ppermute(value, axis, pairs)


def block_length(local_rows, patches):
    shards = 1
    while shards * 2 * local_rows <= 4096 and patches % (shards * 2) == 0:
        shards = shards * 2
    return shards * local_rows


def on_device(
    queries, fresh_keys, fresh_values, stale_keys, stale_values, hidden, out_weight, modulation
):
    query_rows = queries[0]
    keys_fresh = fresh_keys[0]
    values_fresh = fresh_values[0]
    local_rows = query_rows.shape[0]
    head_width = query_rows.shape[1]
    patches = lax.axis_size("patch")
    own_start = lax.axis_index("patch") * local_rows
    score_scale = 1.0 / math.sqrt(head_width)
    block_size = block_length(local_rows, patches)

    def refresh(piece_keys, piece_values, first_row):
        piece_rows = piece_keys.shape[0]
        position = first_row + jnp.arange(piece_rows, dtype=jnp.int32)
        inside = (position >= own_start) & (position < own_start + local_rows)
        offset = jnp.clip(position - own_start, 0, local_rows - 1)
        new_keys = jnp.where(inside[:, None], jnp.take(keys_fresh, offset, axis=0), piece_keys)
        new_values = jnp.where(
            inside[:, None], jnp.take(values_fresh, offset, axis=0), piece_values
        )
        return (new_keys, new_values)

    def attend_block(running, piece_keys, piece_values, first_row):
        running_max, running_sum, running_acc = running
        piece_keys, piece_values = refresh(piece_keys, piece_values, first_row)
        scores = (
            lax.dot_general(
                query_rows, piece_keys, (((1,), (1,)), ((), ())), preferred_element_type=jnp.float32
            )
            * score_scale
        )
        new_max = jnp.maximum(running_max, jnp.max(scores, axis=1))
        factor = jnp.exp(running_max - new_max)
        weights = jnp.exp(scores - new_max[:, None]).astype(jnp.bfloat16)
        new_sum = running_sum * factor + jnp.sum(weights.astype(jnp.float32), axis=1)
        new_acc = running_acc * factor[:, None] + jnp.dot(
            weights, piece_values, preferred_element_type=jnp.float32
        )
        return (new_max, new_sum, new_acc)

    initial = (
        jnp.full((local_rows,), -1e30, jnp.float32),
        jnp.zeros((local_rows,), jnp.float32),
        jnp.zeros((local_rows, head_width), jnp.float32),
    )
    all_keys, all_values = (
        lax.all_gather(stale_keys[0], "patch", axis=0, tiled=True),
        lax.all_gather(stale_values[0], "patch", axis=0, tiled=True),
    )
    running = initial
    piece_keys = all_keys
    piece_values = all_values
    piece_rows = piece_keys.shape[0]
    step_rows = math.gcd(piece_rows, block_size)
    step_count = piece_rows // step_rows
    grouped_keys = piece_keys.reshape(step_count, step_rows, head_width)
    grouped_values = piece_values.reshape(step_count, step_rows, head_width)

    def advance(current, element):
        number, block_keys, block_values = element
        return (attend_block(current, block_keys, block_values, number * step_rows), None)

    running, unused = lax.scan(
        advance, running, (jnp.arange(step_count, dtype=jnp.int32), grouped_keys, grouped_values)
    )
    attention = (running[2] / running[1][:, None]).astype(jnp.bfloat16)
    projected = jnp.dot(attention, out_weight, preferred_element_type=jnp.float32)
    branch_out = (hidden[0].astype(jnp.float32) + modulation[None, :] * projected).astype(
        jnp.bfloat16
    )
    half_width = branch_out.shape[1] // 2
    side = lax.axis_index("guide")
    partner = swapped(branch_out, "guide", 0)
    conditional = jnp.where(side == 0, branch_out, partner)
    unconditional = jnp.where(side == 0, partner, branch_out)
    conditional = lax.dynamic_slice_in_dim(conditional, side * half_width, half_width, 1)
    unconditional = lax.dynamic_slice_in_dim(unconditional, side * half_width, half_width, 1)
    cond_value = conditional.astype(jnp.float32)
    uncond_value = unconditional.astype(jnp.float32)
    return (uncond_value + GUIDANCE * (cond_value - uncond_value)).astype(jnp.bfloat16)


def solution(mesh):
    in_specs = (
        P("guide", "patch", None),
        P("guide", "patch", None),
        P("guide", "patch", None),
        P("guide", "patch", None),
        P("guide", "patch", None),
        P("guide", "patch", None),
        P(),
        P(),
    )
    out_specs = P("patch", "guide")
    return jax.shard_map(
        on_device, mesh=mesh, in_specs=in_specs, out_specs=out_specs, check_vma=False
    )
```

profile of v0, /device:TPU:1, one launch (start us, length us, event | category | flops | bytes accessed | tf_op | source)
XLA Modules:
  0.0 678.7 jit_solution(15807300499211732269)
XLA Ops:
  8.0 217.2 %all-gather.5.cloned.1.call-done = bf16[1,28672,128]{2,1,0:T(8,128)(2,1)} async-done(((bf16[1,112,128]{2,1,0:T(8,128)(2,1)}), bf16[1,28672,128]{2,1,0:T(8,128)(2,1)}) %all-gather.5.cloned.1.call-update) | async-done | bytes 7340048 | tf_op jit(solution)/shard_map/all_gather | solution.py:72
  225.3 216.4 %all-gather.7.cloned.1.call-done = bf16[1,28672,128]{2,1,0:T(8,128)(2,1)} async-done(((bf16[1,112,128]{2,1,0:T(8,128)(2,1)}), bf16[1,28672,128]{2,1,0:T(8,128)(2,1)}) %all-gather.7.cloned.1.call-update) | async-done | bytes 7340048 | tf_op jit(solution)/shard_map/all_gather | solution.py:73
  441.6 212.1 %while.16 = (s32[]{:T(128)}, f32[112]{0:T(128)S(1)}, f32[112]{0:T(128)S(1)}, f32[112,128]{1,0:T(8,128)S(1)}, s32[8]{0:T(128)S(1)}, /*index=5*/s32[]{:T(128)}, s3...) while((s32[]{:T(128)}, f32[112]{0:T(128)S(1)}, ...), condition=%wide.region_3.5_spmd.clone, body=%wide.region_0.4_spmd.clone.sunk | while | flops 210679344 | bytes 12748057 | solution.py:88
  442.9 8.1 %gather_fusion = bf16[3584,128]{1,0:T(8,128)(2,1)} fusion(bf16[112,128]{1,0:T(8,128)(2,1)S(1)} %copy-done.1, s32[4096]{0:T(1024)S(1)} %pad_clamp_fusion.2), kind=kCustom, calls=%fused_computation.clone.clone.1 | custom fusion | bytes 1849344 | tf_op jit(solution)/shard_map/while/body/eval_jaxpr/jit(_take)/gather | solution.py:42
  451.0 4.5 fusion.35
  456.2 8.1 %gather_fusion.1 = bf16[3584,128]{1,0:T(8,128)(2,1)} fusion(bf16[112,128]{1,0:T(8,128)(2,1)S(1)} %copy-done.2, s32[4096]{0:T(1024)S(1)} %pad_clamp_fusion.2), kind=kCustom, calls=%fused_computation.1.clone.clone.1 | custom fusion | bytes 1849344 | tf_op jit(solution)/shard_map/while/body/eval_jaxpr/jit(_take)/gather | solution.py:44
  469.4 8.1 %gather_fusion = bf16[3584,128]{1,0:T(8,128)(2,1)} fusion(bf16[112,128]{1,0:T(8,128)(2,1)S(1)} %copy-done.1, s32[4096]{0:T(1024)S(1)} %pad_clamp_fusion.2), kind=kCustom, calls=%fused_computation.clone.clone.1 | custom fusion | bytes 1849344 | tf_op jit(solution)/shard_map/while/body/eval_jaxpr/jit(_take)/gather | solution.py:42
  477.5 4.5 fusion.35
  482.7 8.1 %gather_fusion.1 = bf16[3584,128]{1,0:T(8,128)(2,1)} fusion(bf16[112,128]{1,0:T(8,128)(2,1)S(1)} %copy-done.2, s32[4096]{0:T(1024)S(1)} %pad_clamp_fusion.2), kind=kCustom, calls=%fused_computation.1.clone.clone.1 | custom fusion | bytes 1849344 | tf_op jit(solution)/shard_map/while/body/eval_jaxpr/jit(_take)/gather | solution.py:44
  490.9 3.8 convolution_add_fusion.2
  495.9 8.1 %gather_fusion = bf16[3584,128]{1,0:T(8,128)(2,1)} fusion(bf16[112,128]{1,0:T(8,128)(2,1)S(1)} %copy-done.1, s32[4096]{0:T(1024)S(1)} %pad_clamp_fusion.2), kind=kCustom, calls=%fused_computation.clone.clone.1 | custom fusion | bytes 1849344 | tf_op jit(solution)/shard_map/while/body/eval_jaxpr/jit(_take)/gather | solution.py:42
  504.0 4.5 fusion.35
  509.3 8.1 %gather_fusion.1 = bf16[3584,128]{1,0:T(8,128)(2,1)} fusion(bf16[112,128]{1,0:T(8,128)(2,1)S(1)} %copy-done.2, s32[4096]{0:T(1024)S(1)} %pad_clamp_fusion.2), kind=kCustom, calls=%fused_computation.1.clone.clone.1 | custom fusion | bytes 1849344 | tf_op jit(solution)/shard_map/while/body/eval_jaxpr/jit(_take)/gather | solution.py:44
  517.4 3.8 convolution_add_fusion.2
  522.4 8.1 %gather_fusion = bf16[3584,128]{1,0:T(8,128)(2,1)} fusion(bf16[112,128]{1,0:T(8,128)(2,1)S(1)} %copy-done.1, s32[4096]{0:T(1024)S(1)} %pad_clamp_fusion.2), kind=kCustom, calls=%fused_computation.clone.clone.1 | custom fusion | bytes 1849344 | tf_op jit(solution)/shard_map/while/body/eval_jaxpr/jit(_take)/gather | solution.py:42
  530.6 4.5 fusion.35
  535.8 8.1 %gather_fusion.1 = bf16[3584,128]{1,0:T(8,128)(2,1)} fusion(bf16[112,128]{1,0:T(8,128)(2,1)S(1)} %copy-done.2, s32[4096]{0:T(1024)S(1)} %pad_clamp_fusion.2), kind=kCustom, calls=%fused_computation.1.clone.clone.1 | custom fusion | bytes 1849344 | tf_op jit(solution)/shard_map/while/body/eval_jaxpr/jit(_take)/gather | solution.py:44
  548.9 8.1 %gather_fusion = bf16[3584,128]{1,0:T(8,128)(2,1)} fusion(bf16[112,128]{1,0:T(8,128)(2,1)S(1)} %copy-done.1, s32[4096]{0:T(1024)S(1)} %pad_clamp_fusion.2), kind=kCustom, calls=%fused_computation.clone.clone.1 | custom fusion | bytes 1849344 | tf_op jit(solution)/shard_map/while/body/eval_jaxpr/jit(_take)/gather | solution.py:42
  557.1 4.5 fusion.35
  562.3 8.1 %gather_fusion.1 = bf16[3584,128]{1,0:T(8,128)(2,1)} fusion(bf16[112,128]{1,0:T(8,128)(2,1)S(1)} %copy-done.2, s32[4096]{0:T(1024)S(1)} %pad_clamp_fusion.2), kind=kCustom, calls=%fused_computation.1.clone.clone.1 | custom fusion | bytes 1849344 | tf_op jit(solution)/shard_map/while/body/eval_jaxpr/jit(_take)/gather | solution.py:44
  575.5 8.1 %gather_fusion = bf16[3584,128]{1,0:T(8,128)(2,1)} fusion(bf16[112,128]{1,0:T(8,128)(2,1)S(1)} %copy-done.1, s32[4096]{0:T(1024)S(1)} %pad_clamp_fusion.2), kind=kCustom, calls=%fused_computation.clone.clone.1 | custom fusion | bytes 1849344 | tf_op jit(solution)/shard_map/while/body/eval_jaxpr/jit(_take)/gather | solution.py:42
  583.6 4.5 fusion.35
  588.8 8.1 %gather_fusion.1 = bf16[3584,128]{1,0:T(8,128)(2,1)} fusion(bf16[112,128]{1,0:T(8,128)(2,1)S(1)} %copy-done.2, s32[4096]{0:T(1024)S(1)} %pad_clamp_fusion.2), kind=kCustom, calls=%fused_computation.1.clone.clone.1 | custom fusion | bytes 1849344 | tf_op jit(solution)/shard_map/while/body/eval_jaxpr/jit(_take)/gather | solution.py:44
  596.9 3.8 convolution_add_fusion.2
  602.0 8.1 %gather_fusion = bf16[3584,128]{1,0:T(8,128)(2,1)} fusion(bf16[112,128]{1,0:T(8,128)(2,1)S(1)} %copy-done.1, s32[4096]{0:T(1024)S(1)} %pad_clamp_fusion.2), kind=kCustom, calls=%fused_computation.clone.clone.1 | custom fusion | bytes 1849344 | tf_op jit(solution)/shard_map/while/body/eval_jaxpr/jit(_take)/gather | solution.py:42
  610.1 4.5 fusion.35
  615.3 8.1 %gather_fusion.1 = bf16[3584,128]{1,0:T(8,128)(2,1)} fusion(bf16[112,128]{1,0:T(8,128)(2,1)S(1)} %copy-done.2, s32[4096]{0:T(1024)S(1)} %pad_clamp_fusion.2), kind=kCustom, calls=%fused_computation.1.clone.clone.1 | custom fusion | bytes 1849344 | tf_op jit(solution)/shard_map/while/body/eval_jaxpr/jit(_take)/gather | solution.py:44
  623.5 3.8 convolution_add_fusion.2
  628.5 8.1 %gather_fusion = bf16[3584,128]{1,0:T(8,128)(2,1)} fusion(bf16[112,128]{1,0:T(8,128)(2,1)S(1)} %copy-done.1, s32[4096]{0:T(1024)S(1)} %pad_clamp_fusion.2), kind=kCustom, calls=%fused_computation.clone.clone.1 | custom fusion | bytes 1849344 | tf_op jit(solution)/shard_map/while/body/eval_jaxpr/jit(_take)/gather | solution.py:42
  636.6 4.5 fusion.35
  641.8 8.1 %gather_fusion.1 = bf16[3584,128]{1,0:T(8,128)(2,1)} fusion(bf16[112,128]{1,0:T(8,128)(2,1)S(1)} %copy-done.2, s32[4096]{0:T(1024)S(1)} %pad_clamp_fusion.2), kind=kCustom, calls=%fused_computation.1.clone.clone.1 | custom fusion | bytes 1849344 | tf_op jit(solution)/shard_map/while/body/eval_jaxpr/jit(_take)/gather | solution.py:44
  655.6 11.6 %collective-permute-start = (bf16[112,5120]{1,0:T(8,128)(2,1)S(1)}, bf16[112,5120]{1,0:T(8,128)(2,1)}, u32[]{:S(2)}, u32[]{:S(2)}) collective-permute-start(bf16[112,5120]{1,0:T(8,128)(2,1)S(1)} %fusion.21), channel_id=1, source_target_pairs={{0,256},{256,0},{1,257},{257,1},{2,258},{258,2},{3,259},{259,3},{4... | collective-permute-start | bytes 3440648 | tf_op jit(solution)/shard_map/ppermute | solution.py:14
  (131 shorter events, 33.9 us)
Async XLA Ops:
  6.5 647.2 %copy-start = (bf16[128,5120]{1,0:T(8,128)(2,1)S(1)}, bf16[128,5120]{1,0:T(8,128)(2,1)}, u32[]{:S(2)}) copy-start(bf16[128,5120]{1,0:T(8,128)(2,1)} %param.18) | copy-start | bytes 3932164
  6.5 218.7 %all-gather.5.cloned.1.call-start = ((), (), s32[]{:S(2)}) async-start(), calls=%async_computation | async-start | bytes 7368704 | tf_op jit(solution)/shard_map/all_gather | solution.py:72
  7.3 434.4 %all-gather.7.cloned.1.call-start = ((), (), s32[]{:S(2)}) async-start(), calls=%async_computation.1 | async-start | bytes 7368704 | tf_op jit(solution)/shard_map/all_gather | solution.py:73
  441.6 212.1 %copy-start.3 = (f32[5120]{0:T(1024)S(1)}, f32[5120]{0:T(1024)}, u32[]{:S(2)}) copy-start(f32[5120]{0:T(1024)} %param.19) | copy-start | bytes 61444
  441.6 1.2 copy-start.1
  442.9 8.2 %copy-start.4 = (bf16[112,128]{1,0:T(8,128)(2,1)S(1)}, bf16[112,128]{1,0:T(8,128)(2,1)}, u32[]{:S(2)}) copy-start(bf16[112,128]{1,0:T(8,128)(2,1)} %get-tuple-element.308) | copy-start | bytes 86020 | tf_op jit(solution)/shard_map/while
  455.5 0.8 copy-start.2
  468.1 1.2 copy-start.1
  469.4 8.2 %copy-start.4 = (bf16[112,128]{1,0:T(8,128)(2,1)S(1)}, bf16[112,128]{1,0:T(8,128)(2,1)}, u32[]{:S(2)}) copy-start(bf16[112,128]{1,0:T(8,128)(2,1)} %get-tuple-element.308) | copy-start | bytes 86020 | tf_op jit(solution)/shard_map/while
  482.0 0.8 copy-start.2
  494.7 1.2 copy-start.1
  495.9 8.2 %copy-start.4 = (bf16[112,128]{1,0:T(8,128)(2,1)S(1)}, bf16[112,128]{1,0:T(8,128)(2,1)}, u32[]{:S(2)}) copy-start(bf16[112,128]{1,0:T(8,128)(2,1)} %get-tuple-element.308) | copy-start | bytes 86020 | tf_op jit(solution)/shard_map/while
  508.5 0.8 copy-start.2
  521.2 1.2 copy-start.1
  522.4 8.2 %copy-start.4 = (bf16[112,128]{1,0:T(8,128)(2,1)S(1)}, bf16[112,128]{1,0:T(8,128)(2,1)}, u32[]{:S(2)}) copy-start(bf16[112,128]{1,0:T(8,128)(2,1)} %get-tuple-element.308) | copy-start | bytes 86020 | tf_op jit(solution)/shard_map/while
  535.0 0.8 copy-start.2
  547.7 1.2 copy-start.1
  548.9 8.2 %copy-start.4 = (bf16[112,128]{1,0:T(8,128)(2,1)S(1)}, bf16[112,128]{1,0:T(8,128)(2,1)}, u32[]{:S(2)}) copy-start(bf16[112,128]{1,0:T(8,128)(2,1)} %get-tuple-element.308) | copy-start | bytes 86020 | tf_op jit(solution)/shard_map/while
  561.5 0.8 copy-start.2
  574.2 1.2 copy-start.1
  575.4 8.2 %copy-start.4 = (bf16[112,128]{1,0:T(8,128)(2,1)S(1)}, bf16[112,128]{1,0:T(8,128)(2,1)}, u32[]{:S(2)}) copy-start(bf16[112,128]{1,0:T(8,128)(2,1)} %get-tuple-element.308) | copy-start | bytes 86020 | tf_op jit(solution)/shard_map/while
  588.1 0.8 copy-start.2
  600.7 1.2 copy-start.1
  602.0 8.2 %copy-start.4 = (bf16[112,128]{1,0:T(8,128)(2,1)S(1)}, bf16[112,128]{1,0:T(8,128)(2,1)}, u32[]{:S(2)}) copy-start(bf16[112,128]{1,0:T(8,128)(2,1)} %get-tuple-element.308) | copy-start | bytes 86020 | tf_op jit(solution)/shard_map/while
  614.6 0.8 copy-start.2
  627.2 1.2 copy-start.1
  628.5 8.2 %copy-start.4 = (bf16[112,128]{1,0:T(8,128)(2,1)S(1)}, bf16[112,128]{1,0:T(8,128)(2,1)}, u32[]{:S(2)}) copy-start(bf16[112,128]{1,0:T(8,128)(2,1)} %get-tuple-element.308) | copy-start | bytes 86020 | tf_op jit(solution)/shard_map/while
  641.1 0.8 copy-start.2
  655.6 14.1 %collective-permute-start = (bf16[112,5120]{1,0:T(8,128)(2,1)S(1)}, bf16[112,5120]{1,0:T(8,128)(2,1)}, u32[]{:S(2)}, u32[]{:S(2)}) collective-permute-start(bf16[112,5120]{1,0:T(8,128)(2,1)S(1)} %fusion.21), channel_id=1, source_target_pairs={{0,256},{256,0},{1,257},{257,1},{2,258},{258,2},{3,259},{259,3},{4... | collective-permute-start | bytes 3440648 | tf_op jit(solution)/shard_map/ppermute | solution.py:14
Sparse Core Ops, SparseCore 0:
  11.7 213.5 all-gather.4
  229.6 211.9 all-gather.6
where the time goes:
time: 680 us; the launch traced here: 679 us
  waiting for transfers between devices  438 us (64%)
  local copies, waits for them, and re-layouts  138 us (20%)
  matrix products  67.4 us (10%)
  between operations  13.5 us (2%)
  starting transfers between devices  11.6 us (2%)
    all_gather x1, waiting for transfers between devices, on_device(): lax.all_gather(stale_keys[0], 'patch', axis=0, tiled=True)  217 us
    all_gather x1, waiting for transfers between devices, on_device(): lax.all_gather(stale_values[0], 'patch', axis=0, tiled=True)  216 us
    gather x8, local copies, waits for them, and re-layouts, refresh(): jnp.take(keys_fresh, offset, axis=0)  65.1 us
    gather x8, local copies, waits for them, and re-layouts, refresh(): jnp.take(values_fresh, offset, axis=0)  65 us
    dot_general x8, matrix products, attend_block(): lax.dot_general(query_rows, piece_keys, (((1,), (1,)), ((), ())), preferr...  35.6 us
    dot_general x8, matrix products, attend_block(): jnp.dot(weights, piece_values, preferred_element_type=jnp.float32)  30 us
  transfers between devices with their start and end apart: 3, of which 3 were waited for; matrix products, arithmetic and copies ran while one was open for 0% of the time, Pallas kernels for 0%

commit v1 on v0

v1 whole, which is shorter than its diff:
```python
import functools
import math

import jax
import jax.numpy as jnp
from jax import lax
from jax.experimental import pallas as pl
from jax.experimental.pallas import tpu as pltpu
from jax.sharding import Mesh
from jax.sharding import PartitionSpec as P

GUIDANCE = 5.0
AXES = ("x", "y", "z")
SIZES = (4, 4, 16)
QUERY_AXES = ("x", "y")
KEY_AXES = ("z",)
STATS = 16


def attend_kernel(place, query, cached, fresh, out, keys, values):
    step = pl.program_id(0)
    steps = pl.num_programs(0)
    rows = query.shape[1]
    head = query.shape[2]
    scale = 1.0 / math.sqrt(head)

    @pl.when(step == 0)
    def _():
        keys[...] = cached[:, :head]
        values[:, :head] = cached[:, head:]
        values[:, head:] = jnp.ones((values.shape[0], head), values.dtype)

    @pl.when(step == steps - 1)
    def _():
        own = pl.ds(pl.multiple_of(place[1] * rows, rows), rows)
        keys[own, :] = fresh[:, :head]
        values[own, :head] = fresh[:, head:]

    scores = lax.dot_general(
        query[0], keys[...], (((1,), (1,)), ((), ())), preferred_element_type=jnp.float32
    )
    peak = jnp.max(scores, axis=1, keepdims=True)
    weights = jnp.exp2((scores - peak) * (scale * math.log2(math.e))).astype(jnp.bfloat16)
    summed = jnp.dot(weights, values[...], preferred_element_type=jnp.float32)
    total = summed[:, head:]
    out[0, :rows, :] = (summed[:, :head] / total).astype(out.dtype)
    level = peak * scale + jnp.log(total)
    level = jnp.concatenate([level, jnp.zeros((head - rows, head), jnp.float32)], axis=0)
    level = level.T[:STATS]
    high = level.astype(jnp.bfloat16).astype(jnp.float32)
    middle = (level - high).astype(jnp.bfloat16).astype(jnp.float32)
    low = level - high - middle
    row = lax.broadcasted_iota(jnp.int32, level.shape, 0)
    stats = jnp.where(row == 0, high, jnp.where(row == 1, middle, low))
    out[0, rows:, :] = stats.astype(out.dtype)


def attend(place, queries, cached, fresh):
    steps, rows, head = queries.shape
    key_rows = cached.shape[0]

    def turn(step, place):
        return (lax.rem(place[0] + 1 + step, steps), 0, 0)

    return pl.pallas_call(
        attend_kernel,
        out_shape=jax.ShapeDtypeStruct((steps, rows + STATS, head), jnp.bfloat16),
        grid_spec=pltpu.PrefetchScalarGridSpec(
            num_scalar_prefetch=1,
            grid=(steps,),
            in_specs=[
                pl.BlockSpec((1, rows, head), turn),
                pl.BlockSpec((key_rows, 2 * head), lambda step, place: (0, 0)),
                pl.BlockSpec((rows, 2 * head), lambda step, place: (0, 0)),
            ],
            out_specs=pl.BlockSpec((1, rows + STATS, head), turn),
            scratch_shapes=[
                pltpu.VMEM((key_rows, head), jnp.bfloat16),
                pltpu.VMEM((key_rows, 2 * head), jnp.bfloat16),
            ],
        ),
        compiler_params=pltpu.CompilerParams(dimension_semantics=("arbitrary",)),
        name="attend",
    )(place, queries, cached, fresh)


def project(attention, hidden, weight, gain):
    projected = jnp.dot(attention, weight, preferred_element_type=jnp.float32)
    return (hidden.astype(jnp.float32) + gain * projected).astype(jnp.bfloat16)


def merge_kernel(place, parts, hidden, weight, gain, attention, out):
    count = parts.shape[0]
    rows = hidden.shape[0]
    head = parts.shape[2]
    levels = []
    for part in range(count):
        pieces = parts[part, rows:, :].astype(jnp.float32)
        levels.append(pieces[0:1] + pieces[1:2] + pieces[2:3])
    level = jnp.concatenate(levels, axis=0)
    share = jnp.exp(level - jnp.max(level, axis=0, keepdims=True))
    share = share / jnp.sum(share, axis=0, keepdims=True)
    share = jnp.concatenate([share, jnp.zeros((head - count, head), jnp.float32)], axis=0).T
    merged = jnp.zeros((rows, head), jnp.float32)
    for part in range(count):
        merged += parts[part, :rows, :].astype(jnp.float32) * share[:rows, part : part + 1]
    merged = merged.astype(jnp.bfloat16)
    attention[...] = merged
    out[...] = project(merged, hidden[...], weight[...], gain[...])


def merge(place, parts, hidden, weight, gain):
    count, padded, head = parts.shape
    rows, width = hidden.shape
    half = width // 2

    def other(step, place):
        return (0, 1 - place[2])

    return pl.pallas_call(
        merge_kernel,
        out_shape=[
            jax.ShapeDtypeStruct((rows, head), jnp.bfloat16),
            jax.ShapeDtypeStruct((rows, half), jnp.bfloat16),
        ],
        grid_spec=pltpu.PrefetchScalarGridSpec(
            num_scalar_prefetch=1,
            grid=(1,),
            in_specs=[
                pl.BlockSpec((count, padded, head), lambda step, place: (0, 0, 0)),
                pl.BlockSpec((rows, half), other),
                pl.BlockSpec((head, half), other),
                pl.BlockSpec((1, half), other),
            ],
            out_specs=[
                pl.BlockSpec((rows, head), lambda step, place: (0, 0)),
                pl.BlockSpec((rows, half), lambda step, place: (0, 0)),
            ],
        ),
        name="merge",
    )(place, parts, hidden, weight, gain)


def own_kernel(place, attention, hidden, weight, gain, out):
    out[...] = project(attention[...], hidden[...], weight[...], gain[...])


def own_half(place, attention, hidden, weight, gain):
    rows, width = hidden.shape
    head = attention.shape[1]
    half = width // 2

    def mine(step, place):
        return (0, place[2])

    return pl.pallas_call(
        own_kernel,
        out_shape=jax.ShapeDtypeStruct((rows, half), jnp.bfloat16),
        grid_spec=pltpu.PrefetchScalarGridSpec(
            num_scalar_prefetch=1,
            grid=(1,),
            in_specs=[
                pl.BlockSpec((rows, head), lambda step, place: (0, 0)),
                pl.BlockSpec((rows, half), mine),
                pl.BlockSpec((head, half), mine),
                pl.BlockSpec((1, half), mine),
            ],
            out_specs=pl.BlockSpec((rows, half), lambda step, place: (0, 0)),
        ),
        cost_estimate=pl.CostEstimate(
            flops=2 * rows * head * half, bytes_accessed=4 * rows * half, transcendentals=0
        ),
        name="own_half",
    )(place, attention, hidden, weight, gain)


def on_device(
    queries, fresh_keys, fresh_values, stale_keys, stale_values, hidden, out_weight, modulation
):
    side = lax.axis_index("guide")
    place = jnp.stack(
        [lax.axis_index(QUERY_AXES), lax.axis_index(KEY_AXES), side]
    ).astype(jnp.int32)
    query_group = lax.axis_size(QUERY_AXES)
    cached = jnp.concatenate([stale_keys[0], stale_values[0]], axis=1)
    fresh = jnp.concatenate([fresh_keys[0], fresh_values[0]], axis=1)
    spread = jnp.broadcast_to(queries, (query_group,) + queries.shape[1:])
    group_queries = lax.all_to_all(spread, QUERY_AXES, 0, 0)
    group_cached = lax.all_gather(cached, KEY_AXES, axis=0, tiled=True)
    partials = attend(place, group_queries, group_cached, fresh)
    parts = lax.all_to_all(partials, QUERY_AXES, 0, 0)
    gain = modulation[None, :]
    attention, sent = merge(place, parts, hidden[0], out_weight, gain)
    partner = lax.ppermute(sent, "guide", [(0, 1), (1, 0)])
    own = own_half(place, attention, hidden[0], out_weight, gain)
    own_value = own.astype(jnp.float32)
    partner_value = partner.astype(jnp.float32)
    conditional = jnp.where(side == 0, own_value, partner_value)
    unconditional = jnp.where(side == 0, partner_value, own_value)
    return (unconditional + GUIDANCE * (conditional - unconditional)).astype(jnp.bfloat16)


def solution(mesh):
    split = Mesh(mesh.devices.reshape((mesh.shape["guide"],) + SIZES), ("guide",) + AXES)
    rows = P("guide", AXES, None)
    return jax.shard_map(
        on_device,
        mesh=split,
        in_specs=(rows,) * 6 + (P(), P()),
        out_specs=P(AXES, "guide"),
        check_vma=False,
    )
```

time: 680 us -> 101 us (0.15)
  waiting for transfers between devices: 438 us -> 0.01 us
  local copies, waits for them, and re-layouts: 138 us -> 2.43 us
  matrix products: 67.4 us -> 0 us
  blocking collectives: 0 us -> 51.9 us
  Pallas kernels: 0 us -> 23.2 us
  between operations: 13.5 us -> 0.07 us
  starting transfers between devices: 11.6 us -> 19.1 us
    all_gather x2 -> x0, waiting for transfers between devices: 434 us -> none  [the longest x1 217 us: on_device(): lax.all_gather(stale_keys[0], 'patch', axis=0, tiled=True)]
    gather x16 -> x0, local copies, waits for them, and re-layouts: 130 us -> none  [the longest x8 65.1 us: refresh(): jnp.take(keys_fresh, offset, axis=0)]
    dot_general x17 -> x0, matrix products: 67.4 us -> none  [the longest x8 35.6 us: attend_block(): lax.dot_general(query_rows, piece_keys, (((1,), (1,)), ((), ())), preferr...]
    all_gather x0 -> x1, blocking collectives: none -> 36.2 us  [on_device(): group_cached = lax.all_gather(cached, KEY_AXES, axis=0, tiled=True)]
    pallas_call x0 -> x3, Pallas kernels: none -> 23.2 us  [the longest x1 16.4 us: attend(): pl.pallas_call(attend_kernel, out_shape=jax.ShapeDtypeStruct((steps, rows...]
    all_to_all x0 -> x1, blocking collectives: none -> 15.7 us  [on_device(): parts = lax.all_to_all(partials, QUERY_AXES, 0, 0)]
    all_to_all x0 -> x1, starting transfers between devices: none -> 7.57 us  [on_device(): group_queries = lax.all_to_all(spread, QUERY_AXES, 0, 0)]
  transfers between devices with their start and end apart: 3 -> 2, of which waited for: 3 -> 0; matrix products, arithmetic and copies ran while one was open for 0% -> 1% of each run, Pallas kernels for 0% -> 3%
where the time goes in v1:
time: 101 us; the launch traced here: 100 us
  blocking collectives  51.9 us (51%)
  Pallas kernels  23.2 us (23%)
  starting transfers between devices  19.1 us (19%)
  other arithmetic  3.4 us (3%)
  local copies, waits for them, and re-layouts  2.43 us (2%)
    all_gather x1, blocking collectives, on_device(): group_cached = lax.all_gather(cached, KEY_AXES, axis=0, tiled=True)  36.2 us
    pallas_call x1, Pallas kernels, attend(): pl.pallas_call(attend_kernel, out_shape=jax.ShapeDtypeStruct((steps, rows...  16.4 us
    all_to_all x1, blocking collectives, on_device(): parts = lax.all_to_all(partials, QUERY_AXES, 0, 0)  15.7 us
    ppermute x1, starting transfers between devices, on_device(): partner = lax.ppermute(sent, 'guide', [(0, 1), (1, 0)])  11.6 us
    all_to_all x1, starting transfers between devices, on_device(): group_queries = lax.all_to_all(spread, QUERY_AXES, 0, 0)  7.57 us
    pallas_call x1, Pallas kernels, merge(): pl.pallas_call(merge_kernel, out_shape=[jax.ShapeDtypeStruct((rows, head)...  3.71 us
    pallas_call x1, Pallas kernels, own_half(): pl.pallas_call(own_kernel, out_shape=jax.ShapeDtypeStruct((rows, half), j...  3.05 us
    convert_element_type x1, other arithmetic, on_device(): (unconditional + GUIDANCE * (conditional - unconditional)).astype(jnp.bfl...  2.15 us
  transfers between devices with their start and end apart: 2, of which 0 were waited for; matrix products, arithmetic and copies ran while one was open for 1% of the time, Pallas kernels for 3%

profile of v1, /device:TPU:1, one launch (start us, length us, event | category | flops | bytes accessed | tf_op | source)
XLA Modules:
  0.0 100.1 jit_solution(5133269505344849923)
XLA Ops:
  0.0 0.0 copy-start.1
  0.0 0.0 copy-start.2
  0.0 0.0 copy-start.3
  0.0 0.0 copy-start.4
  0.0 1.6 %broadcast_in_dim.11 = bf16[16,112,128]{2,1,0:T(8,128)(2,1)} broadcast(bf16[112,128]{1,0:T(8,128)(2,1)} %bitcast.18), dimensions={1,2} | broadcast | bytes 487424 | tf_op jit(solution)/shard_map/broadcast_in_dim | solution.py:187
  1.6 7.6 %all-to-all-start = ((bf16[16,112,128]{2,1,0:T(8,128)(2,1)}), bf16[16,112,128]{2,1,0:T(8,128)(2,1)S(1)}, u32[]{:S(2)}, u32[]{:S(2)}) async-start(bf16[16,112,128]{2,1,0:T(8,128)(2,1)} %broadcast_in_dim.11), calls=%async_computation | async-start | bytes 917504 | tf_op jit(solution)/shard_map/all_to_all | solution.py:188
  9.2 0.0 copy-done.1
  9.2 0.0 copy-done.2
  9.2 0.6 pad_maximum_fusion.1.fresh
  9.9 0.0 copy-done.3
  9.9 0.0 copy-done.4
  9.9 0.6 pad_add_fusion.place
  10.5 36.2 %all_gather.3.cached = bf16[1792,256]{1,0:T(8,128)(2,1)} all-gather(bf16[112,256]{1,0:T(8,128)(2,1)S(1)} %pad_maximum_fusion), channel_id=1, replica_groups=mesh['guide'=2,'x'=4,'y'=4,'z'=16] {'z'}, dimensions={0}, use_global_device_ids=true | all-gather | bytes 974848 | tf_op jit(solution)/shard_map/all_gather | solution.py:189
  46.7 0.0 all-to-all-done.query
  46.8 0.0 copy-start
  46.8 0.8 copy-done
  47.6 16.4 %attend.1 = bf16[16,128,128]{2,1,0:T(8,128)(2,1)} custom-call(s32[3]{0:T(128)} %pad_add_fusion.place, bf16[16,112,128]{2,1,0:T(8,128)(2,1)} %copy-done, bf16[1792,256]{1,0:T(8,128)(2,1)} %all_gather.3.cached, bf16[112,256]{1,0:T(8,128)(2,1)} %pad_maximum_fusion.1.fresh), custom_call_target="tpu_custom_call" | custom-call | tf_op jit(solution)/shard_map/attend/pallas_call | solution.py:65
  64.0 15.7 %all_to_all.10.parts = bf16[16,128,128]{2,1,0:T(8,128)(2,1)} all-to-all(bf16[16,128,128]{2,1,0:T(8,128)(2,1)} %attend.1), channel_id=1, replica_groups=mesh['guide'=2,'x'=4,'y'=4,'z'=16] {'x','y'}, dimensions={0} | all-to-all | bytes 1048576 | tf_op jit(solution)/shard_map/all_to_all | solution.py:191
  79.7 3.7 %merge.1 = (bf16[112,128]{1,0:T(8,128)(2,1)}, bf16[112,2560]{1,0:T(8,128)(2,1)}) custom-call(s32[3]{0:T(128)} %pad_add_fusion.place, bf16[16,128,128]{2,1,0:T(8,128)(2,1)} %all_to_all.10.parts, bf16[112,5120]{1,0:T(8,128)(2,1)} %bitcast.10, bf16[128,5120]{1,0:T(8,128)(2,1)} %weight.3, f32[1,5120]{1,0:T(1,128)} %bitcast.12), custom_call_target="tpu_custom_call" | custom-call | tf_op jit(solution)/shard_map/merge/pallas_call | solution.py:120
  83.4 11.6 %collective-permute-start = (bf16[112,2560]{1,0:T(8,128)(2,1)}, bf16[112,2560]{1,0:T(8,128)(2,1)S(1)}, u32[]{:S(2)}, u32[]{:S(2)}) collective-permute-start(bf16[112,2560]{1,0:T(8,128)(2,1)} %get-tuple-element.7), channel_id=1, source_target_pairs={{0,256},{256,0},{1,257},{257,1},{2,258},{258,2},{3,259},{259,3},{4... | collective-permute-start | bytes 1720328 | tf_op jit(solution)/shard_map/ppermute | solution.py:194
  94.9 3.1 %own_half.1 = bf16[112,2560]{1,0:T(8,128)(2,1)} custom-call(s32[3]{0:T(128)} %pad_add_fusion.place, bf16[112,128]{1,0:T(8,128)(2,1)} %get-tuple-element.8.attention, bf16[112,5120]{1,0:T(8,128)(2,1)} %bitcast.11, bf16[128,5120]{1,0:T(8,128)(2,1)} %weight.3, f32[1,5120]{1,0:T(1,128)} %bitcast.13), custom_call_target="tpu_custom_call" | custom-call | flops 73400320 | bytes 1146880 | tf_op jit(solution)/shard_map/own_half/pallas_call | solution.py:156
  98.0 0.0 collective-permute-done
  98.0 2.1 %fusion.3 = bf16[112,2560]{1,0:T(8,128)(2,1)} fusion(bf16[112,2560]{1,0:T(8,128)(2,1)} %own_half.1, bf16[112,2560]{1,0:T(8,128)(2,1)S(1)} %collective-permute-done, pred[]{:T(512)S(6)} %eq.4), kind=kLoop, calls=%fused_computation.5 | loop fusion | flops 2293760 | bytes 1720321 | tf_op jit(solution)/shard_map/convert_element_type | solution.py:200
  (1 shorter events, 0.0 us)
Async XLA Ops:
  0.0 9.2 %copy-start.1 = (bf16[1,112,128]{2,1,0:T(8,128)(2,1)S(1)}, bf16[1,112,128]{2,1,0:T(8,128)(2,1)}, u32[]{:S(2)}) copy-start(bf16[1,112,128]{2,1,0:T(8,128)(2,1)} %param.10) | copy-start | bytes 86020
  0.0 9.2 %copy-start.2 = (bf16[1,112,128]{2,1,0:T(8,128)(2,1)S(1)}, bf16[1,112,128]{2,1,0:T(8,128)(2,1)}, u32[]{:S(2)}) copy-start(bf16[1,112,128]{2,1,0:T(8,128)(2,1)} %param.9) | copy-start | bytes 86020
  0.0 9.9 %copy-start.3 = (bf16[1,112,128]{2,1,0:T(8,128)(2,1)S(1)}, bf16[1,112,128]{2,1,0:T(8,128)(2,1)}, u32[]{:S(2)}) copy-start(bf16[1,112,128]{2,1,0:T(8,128)(2,1)} %param.12) | copy-start | bytes 86020
  0.0 9.9 %copy-start.4 = (bf16[1,112,128]{2,1,0:T(8,128)(2,1)S(1)}, bf16[1,112,128]{2,1,0:T(8,128)(2,1)}, u32[]{:S(2)}) copy-start(bf16[1,112,128]{2,1,0:T(8,128)(2,1)} %param.11) | copy-start | bytes 86020
  1.6 45.1 %all-to-all-start = ((bf16[16,112,128]{2,1,0:T(8,128)(2,1)}), bf16[16,112,128]{2,1,0:T(8,128)(2,1)S(1)}, u32[]{:S(2)}, u32[]{:S(2)}) async-start(bf16[16,112,128]{2,1,0:T(8,128)(2,1)} %broadcast_in_dim.11), calls=%async_computation | async-start | bytes 917504 | tf_op jit(solution)/shard_map/all_to_all | solution.py:188
  46.8 0.8 copy-start
  83.4 14.6 %collective-permute-start = (bf16[112,2560]{1,0:T(8,128)(2,1)}, bf16[112,2560]{1,0:T(8,128)(2,1)S(1)}, u32[]{:S(2)}, u32[]{:S(2)}) collective-permute-start(bf16[112,2560]{1,0:T(8,128)(2,1)} %get-tuple-element.7), channel_id=1, source_target_pairs={{0,256},{256,0},{1,257},{257,1},{2,258},{258,2},{3,259},{259,3},{4... | collective-permute-start | bytes 1720328 | tf_op jit(solution)/shard_map/ppermute | solution.py:194

commit v2 on v1

v2 whole, which is shorter than its diff:
```python
import math

import jax
import jax.numpy as jnp
from jax import lax
from jax.experimental import pallas as pl
from jax.experimental.pallas import tpu as pltpu
from jax.sharding import Mesh
from jax.sharding import PartitionSpec as P

GUIDANCE = 5.0
AXES = ("x", "y", "z")
SIZES = (4, 4, 16)
QUERY_AXES = ("x", "y")
KEY_AXES = ("z",)
STATS = 16
TOGETHER = 2
VMEM = pl.BlockSpec(memory_space=pltpu.VMEM)
SMEM = pl.BlockSpec(memory_space=pltpu.SMEM)


def write_part(out, index, summed, total, peak, scale):
    rows, head = summed.shape
    out[index, :rows, :] = (summed / total).astype(out.dtype)
    level = peak * scale + jnp.log(total)
    level = jnp.concatenate([level, jnp.zeros((head - rows, head), jnp.float32)], axis=0)
    level = level.T[:STATS]
    high = level.astype(jnp.bfloat16).astype(jnp.float32)
    middle = (level - high).astype(jnp.bfloat16).astype(jnp.float32)
    low = level - high - middle
    row = lax.broadcasted_iota(jnp.int32, level.shape, 0)
    stats = jnp.where(row == 0, high, jnp.where(row == 1, middle, low))
    out[index, rows:, :] = stats.astype(out.dtype)


def prepare_kernel(cached, keys, values):
    head = keys.shape[0]
    keys[...] = cached[:, :head].T
    values[:, :head] = cached[:, head:]
    values[:, head:] = jnp.ones((values.shape[0], head), values.dtype)


def prepare(cached):
    rows, width = cached.shape
    return pl.pallas_call(
        prepare_kernel,
        out_shape=[
            jax.ShapeDtypeStruct((width // 2, rows), cached.dtype),
            jax.ShapeDtypeStruct((rows, width), cached.dtype),
        ],
        in_specs=[VMEM],
        out_specs=[VMEM] * 2,
        compiler_params=pltpu.CompilerParams(vmem_limit_bytes=12 << 20),
        name="prepare",
    )(cached)


def attend_kernel(query, keys, values, out):
    count, rows, head = query.shape
    scale = 1.0 / math.sqrt(head)
    for first in range(0, count, TOGETHER):
        block = query[first : first + TOGETHER].reshape(TOGETHER * rows, head)
        scores = jnp.dot(block, keys[...], preferred_element_type=jnp.float32)
        peak = jnp.max(scores, axis=1, keepdims=True)
        weights = jnp.exp2((scores - peak) * (scale * math.log2(math.e))).astype(jnp.bfloat16)
        summed = jnp.dot(weights, values[...], preferred_element_type=jnp.float32)
        for k in range(TOGETHER):
            part = slice(k * rows, (k + 1) * rows)
            write_part(out, first + k, summed[part, :head], summed[part, head:], peak[part], scale)


def attend(queries, keys, values):
    count, rows, head = queries.shape
    size = count * rows * keys.shape[1]
    return pl.pallas_call(
        attend_kernel,
        out_shape=jax.ShapeDtypeStruct((count, rows + STATS, head), jnp.bfloat16),
        in_specs=[VMEM] * 3,
        out_specs=VMEM,
        cost_estimate=pl.CostEstimate(
            flops=6 * size * head, bytes_accessed=8 * keys.size, transcendentals=size
        ),
        compiler_params=pltpu.CompilerParams(vmem_limit_bytes=24 << 20),
        name="attend",
    )(queries, keys, values)


def attend_own_kernel(place, query, keys, values, fresh, out):
    rows, head = query.shape
    scale = 1.0 / math.sqrt(head)
    contract = (((1,), (1,)), ((), ()))
    stale = jnp.dot(query[...], keys[...], preferred_element_type=jnp.float32)
    column = lax.broadcasted_iota(jnp.int32, stale.shape, 1) - place[1] * rows
    stale = jnp.where((column >= 0) & (column < rows), -jnp.inf, stale)
    new = lax.dot_general(
        query[...], fresh[:, :head], contract, preferred_element_type=jnp.float32
    )
    peak = jnp.maximum(
        jnp.max(stale, axis=1, keepdims=True), jnp.max(new, axis=1, keepdims=True)
    )
    factor = scale * math.log2(math.e)
    stale = jnp.exp2((stale - peak) * factor).astype(jnp.bfloat16)
    new = jnp.exp2((new - peak) * factor).astype(jnp.bfloat16)
    both = jnp.dot(stale, values[...], preferred_element_type=jnp.float32)
    total = both[:, head:] + jnp.sum(new.astype(jnp.float32), axis=1, keepdims=True)
    summed = both[:, :head] + jnp.dot(
        new, fresh[:, head:], preferred_element_type=jnp.float32
    )
    write_part(out, 0, summed, total, peak, scale)


def attend_own(place, query, keys, values, fresh):
    rows, head = query.shape
    size = rows * keys.shape[1]
    return pl.pallas_call(
        attend_own_kernel,
        out_shape=jax.ShapeDtypeStruct((1, rows + STATS, head), jnp.bfloat16),
        in_specs=[SMEM] + [VMEM] * 4,
        out_specs=VMEM,
        cost_estimate=pl.CostEstimate(
            flops=6 * size * head, bytes_accessed=8 * keys.size, transcendentals=size
        ),
        compiler_params=pltpu.CompilerParams(vmem_limit_bytes=12 << 20),
        name="attend_own",
    )(place, query, keys, values, fresh)


def project(attention, hidden, weight, gain):
    projected = jnp.dot(attention, weight, preferred_element_type=jnp.float32)
    return (hidden.astype(jnp.float32) + gain * projected).astype(jnp.bfloat16)


def level_of(part, rows):
    pieces = part[rows:, :].astype(jnp.float32)
    return pieces[0:1] + pieces[1:2] + pieces[2:3]


def merge_kernel(place, parts, own, hidden, weight, gain, attention, out):
    count = parts.shape[0]
    rows = hidden.shape[0]
    head = parts.shape[2]
    levels = []
    for part in range(count):
        level = level_of(parts[part], rows)
        levels.append(jnp.where(place[0] == part, -jnp.inf, level))
    levels.append(level_of(own[0], rows))
    level = jnp.concatenate(levels, axis=0)
    share = jnp.exp(level - jnp.max(level, axis=0, keepdims=True))
    share = share / jnp.sum(share, axis=0, keepdims=True)
    share = jnp.concatenate([share, jnp.zeros((head - count - 1, head), jnp.float32)], axis=0).T
    merged = own[0, :rows, :].astype(jnp.float32) * share[:rows, count : count + 1]
    for part in range(count):
        merged += parts[part, :rows, :].astype(jnp.float32) * share[:rows, part : part + 1]
    merged = merged.astype(jnp.bfloat16)
    attention[...] = merged
    half = out.shape[1]
    other = pl.ds(pl.multiple_of((1 - place[2]) * half, half), half)
    out[...] = project(merged, hidden[:, other], weight[:, other], gain[:, other])


def merge(place, parts, own, hidden, weight, gain):
    rows, width = hidden.shape
    head = parts.shape[2]
    return pl.pallas_call(
        merge_kernel,
        out_shape=[
            jax.ShapeDtypeStruct((rows, head), jnp.bfloat16),
            jax.ShapeDtypeStruct((rows, width // 2), jnp.bfloat16),
        ],
        in_specs=[SMEM] + [VMEM] * 5,
        out_specs=[VMEM] * 2,
        compiler_params=pltpu.CompilerParams(vmem_limit_bytes=12 << 20),
        name="merge",
    )(place, parts, own, hidden, weight, gain)


def own_kernel(place, attention, hidden, weight, gain, out):
    half = out.shape[1]
    mine = pl.ds(pl.multiple_of(place[2] * half, half), half)
    out[...] = project(attention[...], hidden[:, mine], weight[:, mine], gain[:, mine])


def own_half(place, attention, hidden, weight, gain):
    rows, width = hidden.shape
    head = attention.shape[1]
    half = width // 2
    return pl.pallas_call(
        own_kernel,
        out_shape=jax.ShapeDtypeStruct((rows, half), jnp.bfloat16),
        in_specs=[SMEM] + [VMEM] * 4,
        out_specs=VMEM,
        cost_estimate=pl.CostEstimate(
            flops=2 * rows * head * half, bytes_accessed=4 * rows * half, transcendentals=0
        ),
        compiler_params=pltpu.CompilerParams(vmem_limit_bytes=12 << 20),
        name="own_half",
    )(place, attention, hidden, weight, gain)


def exchanged(blocks, axes):
    return lax.all_to_all(blocks, axes, 0, 0)


def spread(block, axes):
    return jnp.broadcast_to(block[None], (lax.axis_size(axes),) + block.shape)


def on_device(
    queries, fresh_keys, fresh_values, stale_keys, stale_values, hidden, out_weight, modulation
):
    side = lax.axis_index("guide")
    place = jnp.stack(
        [lax.axis_index(QUERY_AXES), lax.axis_index(KEY_AXES), side]
    ).astype(jnp.int32)
    query = queries[0]
    residual = hidden[0]
    gain = modulation[None, :]
    cached = jnp.concatenate([stale_keys[0], stale_values[0]], axis=1)
    fresh = jnp.concatenate([fresh_keys[0], fresh_values[0]], axis=1)
    query_blocks = spread(query, QUERY_AXES)
    group_queries = exchanged(query_blocks, QUERY_AXES)
    group_cached = lax.all_gather(cached, KEY_AXES, axis=0, tiled=True)
    keys, values = prepare(group_cached)
    partials = attend(group_queries, keys, values)
    parts = exchanged(partials, QUERY_AXES)
    own_part = attend_own(place, query, keys, values, fresh)
    attention, sent = merge(place, parts, own_part, residual, out_weight, gain)
    partner = lax.ppermute(sent, "guide", [(0, 1), (1, 0)])
    own = own_half(place, attention, residual, out_weight, gain)
    own_value = own.astype(jnp.float32)
    partner_value = partner.astype(jnp.float32)
    conditional = jnp.where(side == 0, own_value, partner_value)
    unconditional = jnp.where(side == 0, partner_value, own_value)
    guided = unconditional + GUIDANCE * (conditional - unconditional)
    return guided.astype(jnp.bfloat16)


def solution(mesh):
    split = Mesh(mesh.devices.reshape((mesh.shape["guide"],) + SIZES), ("guide",) + AXES)
    rows = P("guide", AXES, None)
    return jax.shard_map(
        on_device,
        mesh=split,
        in_specs=(rows,) * 6 + (P(), P()),
        out_specs=P(AXES, "guide"),
        check_vma=False,
    )
```

time: 101 us -> 82.8 us (0.82)
  blocking collectives: 51.9 us -> 34 us
  Pallas kernels: 23.2 us -> 9.84 us
  waiting for transfers between devices: 0.01 us -> 7.37 us
  starting transfers between devices: 19.1 us -> 26.1 us
  other arithmetic: 3.4 us -> 1.18 us
  local copies, waits for them, and re-layouts: 2.43 us -> 3.72 us
    all_to_all x1 -> x0, blocking collectives: 15.7 us -> none  [on_device(): parts = lax.all_to_all(partials, QUERY_AXES, 0, 0)]
    pallas_call x1 -> x3, Pallas kernels: 16.4 us -> 6.78 us  [the longest x1 5.33 us: attend(): pl.pallas_call(attend_kernel, out_shape=jax.ShapeDtypeStruct((count, rows...]
    all_to_all x1 -> x2, starting transfers between devices: 7.57 us -> 14.8 us  [exchanged(): return lax.all_to_all(blocks, axes, 0, 0)]
    all_to_all x1 -> x2, waiting for transfers between devices: 0.01 us -> 6.44 us  [exchanged(): return lax.all_to_all(blocks, axes, 0, 0)]
    pallas_call x1, Pallas kernels: 3.05 us -> 0.85 us  [own_half(): pl.pallas_call(own_kernel, out_shape=jax.ShapeDtypeStruct((rows, half), j...]
    all_gather x1, blocking collectives: 36.2 us -> 34 us  [on_device(): group_cached = lax.all_gather(cached, KEY_AXES, axis=0, tiled=True)]
    pallas_call x1, Pallas kernels: 3.71 us -> 2.21 us  [merge(): pl.pallas_call(merge_kernel, out_shape=[jax.ShapeDtypeStruct((rows, head)...]
    unnamed x10 -> x20, local copies, waits for them, and re-layouts: 0.81 us -> 2.13 us
  transfers between devices with their start and end apart: 2 -> 3, of which waited for: 0 -> 2; matrix products, arithmetic and copies ran while one was open for 1% -> 0% of each run, Pallas kernels for 3% -> 3%
where the time goes in v2:
time: 82.8 us; the launch traced here: 82.4 us
  blocking collectives  34 us (41%)
  starting transfers between devices  26.1 us (32%)
  Pallas kernels  9.84 us (12%)
  waiting for transfers between devices  7.37 us (9%)
  local copies, waits for them, and re-layouts  3.72 us (4%)
  other arithmetic  1.18 us (1%)
    all_gather x1, blocking collectives, on_device(): group_cached = lax.all_gather(cached, KEY_AXES, axis=0, tiled=True)  34 us
    all_to_all x2, starting transfers between devices, exchanged(): return lax.all_to_all(blocks, axes, 0, 0)  14.8 us
    ppermute x1, starting transfers between devices, on_device(): partner = lax.ppermute(sent, 'guide', [(0, 1), (1, 0)])  11.3 us
    all_to_all x2, waiting for transfers between devices, exchanged(): return lax.all_to_all(blocks, axes, 0, 0)  6.44 us
    pallas_call x1, Pallas kernels, attend(): pl.pallas_call(attend_kernel, out_shape=jax.ShapeDtypeStruct((count, rows...  5.33 us
    pallas_call x1, Pallas kernels, merge(): pl.pallas_call(merge_kernel, out_shape=[jax.ShapeDtypeStruct((rows, head)...  2.21 us
    unnamed x20, local copies, waits for them, and re-layouts  2.13 us
  transfers between devices with their start and end apart: 3, of which 2 were waited for; matrix products, arithmetic and copies ran while one was open for 0% of the time, Pallas kernels for 3%

profile of v2, /device:TPU:1, one launch (start us, length us, event | category | flops | bytes accessed | tf_op | source)
XLA Modules:
  0.0 82.4 jit_solution(3467549678325065124)
XLA Ops:
  0.0 0.0 copy-start.7
  0.0 0.0 copy-start.6
  0.0 1.6 %broadcast_in_dim.11 = bf16[16,112,128]{2,1,0:T(8,128)(2,1)} broadcast(bf16[112,128]{1,0:T(8,128)(2,1)} %bitcast.12), dimensions={1,2} | broadcast | bytes 487424 | tf_op jit(solution)/shard_map/broadcast_in_dim | solution.py:205
  1.6 7.6 %all-to-all-start = ((bf16[16,112,128]{2,1,0:T(8,128)(2,1)}), bf16[16,112,128]{2,1,0:T(8,128)(2,1)S(1)}, u32[]{:S(2)}, u32[]{:S(2)}) async-start(bf16[16,112,128]{2,1,0:T(8,128)(2,1)} %broadcast_in_dim.11), calls=%async_computation | async-start | bytes 917504 | tf_op jit(solution)/shard_map/all_to_all | solution.py:201
  9.2 0.0 copy-done.7
  9.2 0.0 copy-done.6
  9.2 34.0 %all_gather.3.cached = bf16[1792,256]{1,0:T(8,128)(2,1)S(1)} all-gather(bf16[112,256]{1,0:T(8,128)(2,1)S(1)} %pad_maximum_fusion), channel_id=1, replica_groups=mesh['guide'=2,'x'=4,'y'=4,'z'=16] {'z'}, dimensions={0}, use_global_device_ids=true | all-gather | bytes 974848 | tf_op jit(solution)/shard_map/all_gather | solution.py:222
  43.3 0.2 prepare.1
  43.5 0.0 all-to-all-done.query
  43.5 0.0 copy-start.8
  43.5 0.0 copy-start.9
  43.5 0.0 copy-start.4
  43.5 0.0 copy-start.5
  43.6 5.3 %attend.1 = bf16[16,128,128]{2,1,0:T(8,128)(2,1)} custom-call(bf16[16,112,128]{2,1,0:T(8,128)(2,1)S(1)} %all-to-all-done.query, bf16[128,1792]{1,0:T(8,128)(2,1)S(1)} %get-tuple-element.9.keys, bf16[1792,256]{1,0:T(8,128)(2,1)S(1)} %get-tuple-element.10.values), custom_call_target="tpu_custom_call" | custom-call | flops 2466250752 | bytes 1835008 | tf_op jit(solution)/shard_map/attend/pallas_call | solution.py:75
  48.9 0.9 %copy-done.2 = bf16[1792,256]{1,0:T(8,128)(2,1)} copy-done((bf16[1792,256]{1,0:T(8,128)(2,1)}, bf16[1792,256]{1,0:T(8,128)(2,1)S(1)}, u32[]{:S(2)}) %copy-start.2) | copy-done | bytes 917528
  49.8 7.2 %all-to-all-start.1 = ((bf16[16,128,128]{2,1,0:T(8,128)(2,1)}), bf16[16,128,128]{2,1,0:T(8,128)(2,1)S(1)}, u32[]{:S(2)}, u32[]{:S(2)}) async-start(bf16[16,128,128]{2,1,0:T(8,128)(2,1)} %attend.1), calls=%async_computation.1 | async-start | bytes 1048576 | tf_op jit(solution)/shard_map/all_to_all | solution.py:201
  57.1 0.1 pad_add_fusion.place
  57.1 0.0 copy-done.8
  57.1 0.0 copy-done.9
  57.2 0.0 copy-done.4
  57.2 0.0 copy-start.3
  57.2 1.2 %copy-done.3 = bf16[1792,256]{1,0:T(8,128)(2,1)S(1)} copy-done((bf16[1792,256]{1,0:T(8,128)(2,1)S(1)}, bf16[1792,256]{1,0:T(8,128)(2,1)}, u32[]{:S(2)}) %copy-start.3) | copy-done | bytes 917528
  58.3 1.2 %attend_own.1.own = bf16[1,128,128]{2,1,0:T(8,128)(2,1)S(1)} custom-call(s32[3]{0:T(128)S(1)} %pad_add_fusion.place, bf16[112,128]{1,0:T(8,128)(2,1)S(1)} %bitcast.13, bf16[128,1792]{1,0:T(8,128)(2,1)S(1)} %get-tuple-element.9.keys, bf16[1792,256]{1,0:T(8,128)(2,1)S(1)} %copy-done.3, bf16[112,256]{1,0:T(8,128)(2,1)S(1)} %pad_maximum_fusion.1.fresh), custom_call_target="tpu_custom_call" | custom-call | flops 154140672 | bytes 1835008 | tf_op jit(solution)/shard_map/attend_own/pallas_call | solution.py:115
  59.6 6.4 %all-to-all-done.1.parts = bf16[16,128,128]{2,1,0:T(8,128)(2,1)S(1)} async-done(((bf16[16,128,128]{2,1,0:T(8,128)(2,1)}), bf16[16,128,128]{2,1,0:T(8,128)(2,1)S(1)}, u32[]{:S(2)}, u32[]{:S(2)}) %all-to-all-start.1) | async-done | bytes 524320 | tf_op jit(solution)/shard_map/all_to_all | solution.py:201
  66.0 0.0 copy-done.5
  66.0 0.0 copy-done
  66.0 0.0 copy-done.1
  66.0 2.2 %merge.1 = (bf16[112,128]{1,0:T(8,128)(2,1)S(1)}, bf16[112,2560]{1,0:T(8,128)(2,1)}) custom-call(s32[3]{0:T(128)S(1)} %pad_add_fusion.place, bf16[16,128,128]{2,1,0:T(8,128)(2,1)S(1)} %all-to-all-done.1.parts, bf16[1,128,128]{2,1,0:T(8,128)(2,1)S(1)} %attend_own.1.own, bf16[112,5120]{1,0:T(8,128)(2,1)S(1)} %bitcast.10, bf16[128,5120]{1,0:T(8,128)(2,1)S(1)} %copy-done, ...), custom_call_target="tpu_custom_call" | custom-call | tf_op jit(solution)/shard_map/merge/pallas_call | solution.py:164
  68.2 11.3 %collective-permute-start = (bf16[112,2560]{1,0:T(8,128)(2,1)}, bf16[112,2560]{1,0:T(8,128)(2,1)S(1)}, u32[]{:S(2)}, u32[]{:S(2)}) collective-permute-start(bf16[112,2560]{1,0:T(8,128)(2,1)} %get-tuple-element.11), channel_id=1, source_target_pairs={{0,256},{256,0},{1,257},{257,1},{2,258},{258,2},{3,259},{259,3},{4... | collective-permute-start | bytes 1720328 | tf_op jit(solution)/shard_map/ppermute | solution.py:228
  79.5 0.9 %own_half.1 = bf16[112,2560]{1,0:T(8,128)(2,1)S(1)} custom-call(s32[3]{0:T(128)S(1)} %pad_add_fusion.place, bf16[112,128]{1,0:T(8,128)(2,1)S(1)} %get-tuple-element.12.attention, bf16[112,5120]{1,0:T(8,128)(2,1)S(1)} %bitcast.11, bf16[128,5120]{1,0:T(8,128)(2,1)S(1)} %copy-done, f32[1,5120]{1,0:T(1,128)S(1)} %bitcast.15), custom_call_target="tpu_custom_call" | custom-call | flops 73400320 | bytes 1146880 | tf_op jit(solution)/shard_map/own_half/pallas_call | solution.py:187
  80.4 0.9 %collective-permute-done = bf16[112,2560]{1,0:T(8,128)(2,1)S(1)} collective-permute-done((bf16[112,2560]{1,0:T(8,128)(2,1)}, bf16[112,2560]{1,0:T(8,128)(2,1)S(1)}, u32[]{:S(2)}, u32[]{:S(2)}) %collective-permute-start) | collective-permute-done | bytes 573472 | tf_op jit(solution)/shard_map/ppermute | solution.py:228
  81.3 1.1 %fusion.3 = bf16[112,2560]{1,0:T(8,128)(2,1)} fusion(bf16[112,2560]{1,0:T(8,128)(2,1)S(1)} %own_half.1, bf16[112,2560]{1,0:T(8,128)(2,1)S(1)} %collective-permute-done, pred[]{:T(512)S(6)} %eq.4), kind=kLoop, calls=%fused_computation.5 | loop fusion | flops 2293760 | bytes 1720321 | tf_op jit(solution)/shard_map/convert_element_type | solution.py:235
  (5 shorter events, 0.0 us)
Async XLA Ops:
  0.0 9.2 %copy-start.7 = (bf16[1,112,128]{2,1,0:T(8,128)(2,1)S(1)}, bf16[1,112,128]{2,1,0:T(8,128)(2,1)}, u32[]{:S(2)}) copy-start(bf16[1,112,128]{2,1,0:T(8,128)(2,1)} %param.11) | copy-start | bytes 86020
  0.0 9.2 %copy-start.6 = (bf16[1,112,128]{2,1,0:T(8,128)(2,1)S(1)}, bf16[1,112,128]{2,1,0:T(8,128)(2,1)}, u32[]{:S(2)}) copy-start(bf16[1,112,128]{2,1,0:T(8,128)(2,1)} %param.12) | copy-start | bytes 86020
  1.6 41.9 %all-to-all-start = ((bf16[16,112,128]{2,1,0:T(8,128)(2,1)}), bf16[16,112,128]{2,1,0:T(8,128)(2,1)S(1)}, u32[]{:S(2)}, u32[]{:S(2)}) async-start(bf16[16,112,128]{2,1,0:T(8,128)(2,1)} %broadcast_in_dim.11), calls=%async_computation | async-start | bytes 917504 | tf_op jit(solution)/shard_map/all_to_all | solution.py:201
  43.5 13.6 %copy-start.8 = (bf16[1,112,128]{2,1,0:T(8,128)(2,1)S(1)}, bf16[1,112,128]{2,1,0:T(8,128)(2,1)}, u32[]{:S(2)}) copy-start(bf16[1,112,128]{2,1,0:T(8,128)(2,1)} %param.10) | copy-start | bytes 86020
  43.5 13.6 %copy-start.9 = (bf16[1,112,128]{2,1,0:T(8,128)(2,1)S(1)}, bf16[1,112,128]{2,1,0:T(8,128)(2,1)}, u32[]{:S(2)}) copy-start(bf16[1,112,128]{2,1,0:T(8,128)(2,1)} %param.9) | copy-start | bytes 86020
  43.5 13.6 %copy-start.4 = (bf16[1,112,128]{2,1,0:T(8,128)(2,1)S(1)}, bf16[1,112,128]{2,1,0:T(8,128)(2,1)}, u32[]{:S(2)}) copy-start(bf16[1,112,128]{2,1,0:T(8,128)(2,1)} %param.8) | copy-start | bytes 86020
  43.5 22.5 %copy-start.5 = (f32[5120]{0:T(1024)S(1)}, f32[5120]{0:T(1024)}, u32[]{:S(2)}) copy-start(f32[5120]{0:T(1024)} %param.15) | copy-start | bytes 61444
  48.9 0.9 %copy-start.2 = (bf16[1792,256]{1,0:T(8,128)(2,1)}, bf16[1792,256]{1,0:T(8,128)(2,1)S(1)}, u32[]{:S(2)}) copy-start(bf16[1792,256]{1,0:T(8,128)(2,1)S(1)} %get-tuple-element.10.values) | copy-start | bytes 2752516
  49.8 16.2 %copy-start = (bf16[128,5120]{1,0:T(8,128)(2,1)S(1)}, bf16[128,5120]{1,0:T(8,128)(2,1)}, u32[]{:S(2)}) copy-start(bf16[128,5120]{1,0:T(8,128)(2,1)} %weight.3) | copy-start | bytes 3932164
  49.8 16.2 %copy-start.1 = (bf16[1,112,5120]{2,1,0:T(8,128)(2,1)S(1)}, bf16[1,112,5120]{2,1,0:T(8,128)(2,1)}, u32[]{:S(2)}) copy-start(bf16[1,112,5120]{2,1,0:T(8,128)(2,1)} %param.13) | copy-start | bytes 3440644
  49.8 16.2 %all-to-all-start.1 = ((bf16[16,128,128]{2,1,0:T(8,128)(2,1)}), bf16[16,128,128]{2,1,0:T(8,128)(2,1)S(1)}, u32[]{:S(2)}, u32[]{:S(2)}) async-start(bf16[16,128,128]{2,1,0:T(8,128)(2,1)} %attend.1), calls=%async_computation.1 | async-start | bytes 1048576 | tf_op jit(solution)/shard_map/all_to_all | solution.py:201
  57.2 1.2 %copy-start.3 = (bf16[1792,256]{1,0:T(8,128)(2,1)S(1)}, bf16[1792,256]{1,0:T(8,128)(2,1)}, u32[]{:S(2)}) copy-start(bf16[1792,256]{1,0:T(8,128)(2,1)} %copy-done.2) | copy-start | bytes 2752516
  68.2 13.1 %collective-permute-start = (bf16[112,2560]{1,0:T(8,128)(2,1)}, bf16[112,2560]{1,0:T(8,128)(2,1)S(1)}, u32[]{:S(2)}, u32[]{:S(2)}) collective-permute-start(bf16[112,2560]{1,0:T(8,128)(2,1)} %get-tuple-element.11), channel_id=1, source_target_pairs={{0,256},{256,0},{1,257},{257,1},{2,258},{258,2},{3,259},{259,3},{4... | collective-permute-start | bytes 1720328 | tf_op jit(solution)/shard_map/ppermute | solution.py:228
